TPU v7x, 128 devices: a whole 4x4x4 slice. The times are simulated.
128 devices in a mesh: map: 16 (over y, x), rep: 8 (over z, core).
Axes of the slice: x: 4, y: 4, z: 4, core: 2. Of those that a mesh axis runs over, the one named last changes fastest.
Arguments:
- amplitudes: float32 [2, 4096, 5120], P(None, ('map', 'rep')), may hold values from -6 to 6
- integrals: float32 [2, 5120, 5120], P(None, None, ('map', 'rep')), may hold values from -0.078125 to 0.078125
- row_gap: float32 [2, 4096], P(None, ('map', 'rep')), may hold values from 0.5 to 4
- col_gap: float32 [2, 5120], replicated, may hold values from 0.5 to 4
Outputs:
- update: float32 [2, 4096, 5120], P(None, ('map', 'rep'))
All inputs are finite; a program needn't handle non-finite values.
Results may differ from a plain program's by a relative error of at most 0.00007.
Values sent between devices are 32-bit elements; how exact they have to be, the bound alone decides.
No kernel may reach another device: no remote copies, remote signals or barrier semaphores. Data moves between devices by JAX's collectives and lax.ppermute only.
A program may use at most 128 MiB of HBM per device.

v0:
```python
import jax
import jax.numpy as jnp
from jax import lax
from jax.sharding import PartitionSpec as P


def per_device(amplitudes, integrals, row_gap, col_gap):
    amp_block = lax.all_to_all(amplitudes, "rep", split_axis=2, concat_axis=1, tiled=True)
    int_block = lax.all_to_all(integrals, "rep", split_axis=1, concat_axis=2, tiled=True)
    partial_value = jnp.einsum(
        "gsk,gkc->gsc",
        amp_block,
        lax.all_gather(int_block, "map", axis=2, tiled=True),
        precision=lax.Precision.HIGHEST,
        preferred_element_type=jnp.float32,
    )
    product = lax.psum_scatter(partial_value, "rep", scatter_dimension=1, tiled=True)
    return product / (row_gap[:, :, None] + col_gap[:, None, :])


def solution(mesh):
    placed = (
        P(None, ("map", "rep"), None),
        P(None, None, ("map", "rep")),
        P(None, ("map", "rep")),
        P(),
    )
    return jax.shard_map(
        per_device,
        mesh=mesh,
        in_specs=placed,
        out_specs=P(None, ("map", "rep"), None),
        check_vma=False,
    )
```

profile of v0, /device:TPU:1, one launch (start us, length us, event | category | flops | bytes accessed | tf_op | source)
XLA Modules:
  0.0 337.0 jit_solution(603539111832813769)
XLA Ops:
  6.5 0.0 all-gather.2.cloned.1.call-start
  6.5 6.9 %copy.9 = f32[2,5120,40]{2,0,1:T(2,128)} copy(f32[2,5120,40]{1,2,0:T(8,128)} %param.5) | data formatting | bytes 3276800 | tf_op args[1]
  13.5 10.8 %reshape.4 = f32[8,1,51200]{2,1,0:T(1,128)S(1)} reshape(f32[5120,2,40]{2,1,0:T(2,128)} %bitcast.17) | data formatting | bytes 3276800
  24.3 28.4 %all_to_all.36 = f32[8,1,51200]{2,1,0:T(1,128)S(1)} all-to-all(f32[8,1,51200]{2,1,0:T(1,128)S(1)} %reshape.4), channel_id=1, replica_groups=mesh['map'=16,'rep'=8] {'rep'}, dimensions={0} | all-to-all | bytes 3276800 | tf_op jit(solution)/shard_map/all_to_all | solution.py:9
  52.7 0.5 broadcast.2
  53.2 4.5 %reduce.1 = f32[8,51200]{1,0:T(8,128)S(1)} reduce(f32[8,1,51200]{2,1,0:T(1,128)S(1)} %all_to_all.36, f32[]{:T(128)} %broadcast.2), dimensions={1}, to_apply=%all_to_all.30.reduce_sub_computation | reduce | bytes 3276804 | tf_op jit(solution)/shard_map/all_to_all | solution.py:9
  57.7 11.4 %reshape.5 = f32[5120,2,40]{2,1,0:T(2,128)} reshape(f32[8,51200]{1,0:T(8,128)S(1)} %reduce.1) | data formatting | bytes 3276800
  69.2 6.9 %copy.10 = f32[2,8,640,40]{2,3,1,0:T(8,128)} copy(f32[2,8,640,40]{3,0,2,1:T(2,128)} %bitcast.16) | data formatting | bytes 3276800 | tf_op jit(solution)/shard_map/all_to_all | solution.py:9
  76.0 0.0 copy-start
  76.0 0.0 all-gather.2.cloned.1.call-update
  76.1 0.2 reduce-scatter.2.cloned.1.call-start
  76.3 1.1 copy-done
  77.4 4.7 %copy.7 = f32[2,32,5120]{1,0,2:T(2,128)} copy(f32[2,32,5120]{2,1,0:T(8,128)S(1)} %copy-done) | data formatting | bytes 2621440 | tf_op args[0]
  82.0 6.8 %reshape.2 = f32[8,1,40960]{2,1,0:T(1,128)S(1)} reshape(f32[5120,2,32]{2,1,0:T(2,128)} %bitcast.15) | data formatting | bytes 2621440
  88.9 21.1 %all_to_all.37 = f32[8,1,40960]{2,1,0:T(1,128)S(1)} all-to-all(f32[8,1,40960]{2,1,0:T(1,128)S(1)} %reshape.2), channel_id=1, replica_groups=mesh['map'=16,'rep'=8] {'rep'}, dimensions={0} | all-to-all | bytes 2621440 | tf_op jit(solution)/shard_map/all_to_all | solution.py:8
  110.0 3.8 %reduce = f32[8,40960]{1,0:T(8,128)S(1)} reduce(f32[8,1,40960]{2,1,0:T(1,128)S(1)} %all_to_all.37, f32[]{:T(128)} %broadcast.2), dimensions={1}, to_apply=%all_to_all.26.reduce_sub_computation | reduce | bytes 2621444 | tf_op jit(solution)/shard_map/all_to_all | solution.py:8
  113.8 6.8 %reshape.3 = f32[5120,2,32]{2,1,0:T(2,128)} reshape(f32[8,40960]{1,0:T(8,128)S(1)} %reduce) | data formatting | bytes 2621440
  120.6 5.5 %copy.8 = f32[2,32,8,640]{3,1,2,0:T(8,128)S(1)} copy(f32[2,32,8,640]{1,0,3,2:T(2,128)} %bitcast.14) | data formatting | bytes 2621440 | tf_op jit(solution)/shard_map/all_to_all | solution.py:8
  126.1 109.1 %all-gather.2.cloned.1.call-done = f32[2,640,5120]{1,2,0:T(8,128)} async-done(((f32[2,640,320]{1,2,0:T(8,128)}), f32[2,640,5120]{1,2,0:T(8,128)}) %all-gather.2.cloned.1.call-update) | async-done | bytes 26214416 | tf_op jit(solution)/shard_map/all_gather | solution.py:13
  235.2 30.5 %fusion = f32[2,256,5120]{2,1,0:T(8,128)} fusion(f32[2,256,640]{2,1,0:T(8,128)S(1)} %bitcast.19, f32[2,640,5120]{1,2,0:T(8,128)} %all-gather.2.cloned.1.call-done), kind=kOutput, calls=%fused_computation.1 | convolution fusion | flops 20132659200 | bytes 38010880 | tf_op jit(solution)/shard_map/gsk,gkc->gsc/dot_general | solution.py:10
  265.7 0.0 copy-start.1
  265.7 0.0 copy-start.2
  265.7 0.0 reduce-scatter.2.cloned.1.call-update
  265.7 61.8 %reduce-scatter.2.cloned.1.call-done = f32[2,32,5120]{2,1,0:T(8,128)} async-done(((f32[2,256,5120]{2,1,0:T(8,128)}), f32[2,32,5120]{2,1,0:T(8,128)}) %reduce-scatter.2.cloned.1.call-update) | async-done | bytes 1310736 | tf_op jit(solution)/shard_map/reduce_scatter | solution.py:17
  327.5 0.0 copy-done.1
  327.5 0.0 copy-done.2
  327.5 2.6 add_divide_fusion
Async XLA Ops:
  6.5 228.7 %all-gather.2.cloned.1.call-start = ((), (), s32[]{:S(2)}) async-start(), calls=%async_computation.3 | async-start | bytes 27852800 | tf_op jit(solution)/shard_map/all_gather | solution.py:13
  76.0 1.3 copy-start
  76.1 251.4 %reduce-scatter.2.cloned.1.call-start = ((), (), s32[]{:S(2)}) async-start(), calls=%async_computation.4 | async-start | bytes 11796480 | tf_op jit(solution)/shard_map/reduce_scatter | solution.py:17
  265.7 61.8 %copy-start.1 = (f32[2,5120]{1,0:T(2,128)S(1)}, f32[2,5120]{1,0:T(2,128)}, u32[]{:S(2)}) copy-start(f32[2,5120]{1,0:T(2,128)} %param.7) | copy-start | bytes 122884
  265.7 61.8 %copy-start.2 = (f32[2,32]{1,0:T(2,128)S(1)}, f32[2,32]{1,0:T(2,128)}, u32[]{:S(2)}) copy-start(f32[2,32]{1,0:T(2,128)} %param.6) | copy-start | bytes 772
Sparse Core Ops, SparseCore 0:
  76.2 158.9 all-gather.1
  265.8 61.6 reduce-scatter.1
where the time goes:
time: 338 us; the launch traced here: 337 us
  waiting for transfers between devices  171 us (51%)
  local copies, waits for them, and re-layouts  61.5 us (18%)
  blocking collectives  49.5 us (15%)
  matrix products  30.5 us (9%)
  between operations  13.4 us (4%)
  other arithmetic  10.9 us (3%)
    all_gather x1, waiting for transfers between devices, per_device(): lax.all_gather(int_block, 'map', axis=2, tiled=True)  109 us
    reduce_scatter x1, waiting for transfers between devices, per_device(): lax.psum_scatter(partial_value, 'rep', scatter_dimension=1, tiled=True)  61.8 us
    unnamed x12, local copies, waits for them, and re-layouts  48.6 us
    dot_general x1, matrix products, per_device(): jnp.einsum('gsk,gkc->gsc', amp_block, lax.all_gather(int_block, 'map', ax...  30.5 us
    all_to_all x1, blocking collectives, per_device(): lax.all_to_all(integrals, 'rep', split_axis=1, concat_axis=2, tiled=True)  28.4 us
    all_to_all x1, blocking collectives, per_device(): lax.all_to_all(amplitudes, 'rep', split_axis=2, concat_axis=1, tiled=True)  21.1 us
    all_to_all x1, local copies, waits for them, and re-layouts, per_device(): lax.all_to_all(integrals, 'rep', split_axis=1, concat_axis=2, tiled=True)  6.88 us
  transfers between devices with their start and end apart: 2, of which 2 were waited for; matrix products, arithmetic and copies ran while one was open for 8% of the time, Pallas kernels for 0%

commit v1 on v0

--- a/solution.py
+++ b/solution.py
@@ -10,7 +10,9 @@
     partial_value = jnp.einsum(
         "gsk,gkc->gsc",
         amp_block,
-        lax.all_gather(int_block, "map", axis=2, tiled=True),
+        jnp.concatenate(
+            lax.all_to_all(jnp.stack([int_block] * lax.axis_size("map")), "map", 0, 0), axis=2
+        ),
         precision=lax.Precision.HIGHEST,
         preferred_element_type=jnp.float32,
     )

time: 338 us -> 603 us (1.78)
  waiting for transfers between devices: 171 us -> 444 us
  blocking collectives: 49.5 us -> 0 us
  local copies, waits for them, and re-layouts: 61.5 us -> 81.3 us
  starting transfers between devices: 0.22 us -> 19.5 us
    all_to_all x0 -> x3, waiting for transfers between devices: none -> 385 us  [the longest x1 376 us: per_device(): lax.all_to_all(jnp.stack([int_block] * lax.axis_size('map')), 'map', 0, 0)]
    all_gather x1 -> x0, waiting for transfers between devices: 109 us -> none  [per_device(): lax.all_gather(int_block, 'map', axis=2, tiled=True)]
    all_to_all x2 -> x0, blocking collectives: 49.5 us -> none  [the longest x1 28.4 us: per_device(): lax.all_to_all(integrals, 'rep', split_axis=1, concat_axis=2, tiled=True)]
    all_to_all x0 -> x3, starting transfers between devices: none -> 19.3 us  [the longest x1 6.95 us: per_device(): lax.all_to_all(integrals, 'rep', split_axis=1, concat_axis=2, tiled=True)]
    another operation x0 -> x1, local copies, waits for them, and re-layouts: none -> 11.6 us  [per_device(): jnp.stack([int_block] * lax.axis_size('map'))]
    all_to_all x0 -> x1, local copies, waits for them, and re-layouts: none -> 9.42 us  [per_device(): lax.all_to_all(jnp.stack([int_block] * lax.axis_size('map')), 'map', 0, 0)]
  transfers between devices with their start and end apart: 2 -> 4, of which waited for: 2 -> 3; matrix products, arithmetic and copies ran while one was open for 8% -> 9% of each run, Pallas kernels for 0% -> 0%
where the time goes in v1:
time: 603 us; the launch traced here: 599 us
  waiting for transfers between devices  444 us (74%)
  local copies, waits for them, and re-layouts  81.3 us (13%)
  matrix products  28.6 us (5%)
  starting transfers between devices  19.5 us (3%)
  between operations  13.7 us (2%)
  other arithmetic  12.3 us (2%)
    all_to_all x1, waiting for transfers between devices, per_device(): lax.all_to_all(jnp.stack([int_block] * lax.axis_size('map')), 'map', 0, 0)  376 us
    reduce_scatter x1, waiting for transfers between devices, per_device(): lax.psum_scatter(partial_value, 'rep', scatter_dimension=1, tiled=True)  58.5 us
    unnamed x12, local copies, waits for them, and re-layouts  48.6 us
    dot_general x1, matrix products, per_device(): jnp.einsum('gsk,gkc->gsc', amp_block, jnp.concatenate(lax.all_to_all(jnp....  28.6 us
  transfers between devices with their start and end apart: 4, of which 3 were waited for; matrix products, arithmetic and copies ran while one was open for 9% of the time, Pallas kernels for 0%

profile of v1, /device:TPU:1, one launch (start us, length us, event | category | flops | bytes accessed | tf_op | source)
XLA Modules:
  0.0 599.4 jit_solution(11074479332016169882)
XLA Ops:
  6.5 6.9 %copy.13 = f32[2,5120,40]{2,0,1:T(2,128)} copy(f32[2,5120,40]{1,2,0:T(8,128)} %param.5) | data formatting | bytes 3276800 | tf_op args[1]
  13.4 11.5 %reshape.15 = f32[8,1,51200]{2,1,0:T(1,128)} reshape(f32[5120,2,40]{2,1,0:T(2,128)} %bitcast.22) | data formatting | bytes 3276800
  25.0 0.0 copy-start
  25.0 6.9 %all-to-all-start.1 = ((f32[8,1,51200]{2,1,0:T(1,128)}), f32[8,1,51200]{2,1,0:T(1,128)S(1)}, u32[]{:S(2)}, u32[]{:S(2)}) async-start(f32[8,1,51200]{2,1,0:T(1,128)} %reshape.15), calls=%async_computation.1 | async-start | bytes 3276800 | tf_op jit(solution)/shard_map/all_to_all | solution.py:9
  31.9 0.0 copy-done
  31.9 4.7 copy.11
  36.6 7.4 %reshape.13 = f32[8,1,40960]{2,1,0:T(1,128)} reshape(f32[5120,2,32]{2,1,0:T(2,128)} %bitcast.20) | data formatting | bytes 2621440
  44.0 9.3 %all-to-all-done.1 = f32[8,1,51200]{2,1,0:T(1,128)S(1)} async-done(((f32[8,1,51200]{2,1,0:T(1,128)}), f32[8,1,51200]{2,1,0:T(1,128)S(1)}, u32[]{:S(2)}, u32[]{:S(2)}) %all-to-all-start.1) | async-done | bytes 1638432 | tf_op jit(solution)/shard_map/all_to_all | solution.py:9
  53.3 5.5 all-to-all-start
  58.9 0.6 broadcast.3
  59.5 4.6 reduce.1
  64.1 11.4 %reshape.16 = f32[5120,2,40]{2,1,0:T(2,128)} reshape(f32[8,51200]{1,0:T(8,128)S(1)} %reduce.1) | data formatting | bytes 3276800
  75.5 5.5 copy.20
  81.0 0.0 all-to-all-done
  81.0 11.6 %stack.5 = f32[16,2,640,320]{2,3,1,0:T(8,128)} broadcast(f32[2,640,320]{1,2,0:T(8,128)S(1)} %bitcast.23), dimensions={1,2,3} | broadcast | bytes 27852800 | tf_op jit(solution)/shard_map/stack | solution.py:14
  92.6 6.8 %all-to-all-start.2 = ((f32[16,2,640,320]{2,3,1,0:T(8,128)}), f32[16,2,640,320]{2,3,1,0:T(8,128)}, u32[]{:S(2)}, u32[]{:S(2)}) async-start(f32[16,2,640,320]{2,3,1,0:T(8,128)} %stack.5), calls=%async_computation.2 | async-start | bytes 52428800 | tf_op jit(solution)/shard_map/all_to_all | solution.py:14
  99.4 0.2 reduce-scatter.2.cloned.1.call-start
  99.6 5.1 reduce
  104.8 6.7 %reshape.14 = f32[5120,2,32]{2,1,0:T(2,128)} reshape(f32[8,40960]{1,0:T(8,128)S(1)} %reduce) | data formatting | bytes 2621440
  111.5 5.5 copy.12
  117.0 376.2 %all-to-all-done.2 = f32[16,2,640,320]{2,3,1,0:T(8,128)} async-done(((f32[16,2,640,320]{2,3,1,0:T(8,128)}), f32[16,2,640,320]{2,3,1,0:T(8,128)}, u32[]{:S(2)}, u32[]{:S(2)}) %all-to-all-start.2) | async-done | bytes 26214432 | tf_op jit(solution)/shard_map/all_to_all | solution.py:14
  493.2 9.4 %copy.16 = f32[16,2,640,320]{2,3,0,1:T(8,128)S(1)} copy(f32[16,2,640,320]{2,3,1,0:T(8,128)} %all-to-all-done.2) | data formatting | bytes 52428800 | tf_op jit(solution)/shard_map/all_to_all | solution.py:14
  502.6 28.6 %fusion = f32[2,256,5120]{2,1,0:T(8,128)} fusion(f32[2,256,640]{2,1,0:T(8,128)S(1)} %bitcast.24, f32[2,640,5120]{1,2,0:T(8,128)S(1)} %bitcast.18), kind=kOutput, calls=%fused_computation.1 | convolution fusion | flops 20132659200 | bytes 38010880 | tf_op jit(solution)/shard_map/gsk,gkc->gsc/dot_general | solution.py:10
  531.2 0.0 copy-start.1
  531.2 0.0 copy-start.2
  531.2 0.0 reduce-scatter.2.cloned.1.call-update
  531.2 58.5 %reduce-scatter.2.cloned.1.call-done = f32[2,32,5120]{2,1,0:T(8,128)} async-done(((f32[2,256,5120]{2,1,0:T(8,128)}), f32[2,32,5120]{2,1,0:T(8,128)}) %reduce-scatter.2.cloned.1.call-update) | async-done | bytes 1310736 | tf_op jit(solution)/shard_map/reduce_scatter | solution.py:19
  589.7 0.0 copy-done.1
  589.7 0.0 copy-done.2
  589.7 2.6 add_divide_fusion
Async XLA Ops:
  25.0 7.0 %copy-start = (f32[2,32,5120]{2,1,0:T(8,128)S(1)}, f32[2,32,5120]{2,1,0:T(8,128)}, u32[]{:S(2)}) copy-start(f32[2,32,5120]{2,1,0:T(8,128)} %param.4) | copy-start | bytes 3932164
  25.0 28.4 %all-to-all-start.1 = ((f32[8,1,51200]{2,1,0:T(1,128)}), f32[8,1,51200]{2,1,0:T(1,128)S(1)}, u32[]{:S(2)}, u32[]{:S(2)}) async-start(f32[8,1,51200]{2,1,0:T(1,128)} %reshape.15), calls=%async_computation.1 | async-start | bytes 3276800 | tf_op jit(solution)/shard_map/all_to_all | solution.py:9
  53.3 27.7 %all-to-all-start = ((f32[8,1,40960]{2,1,0:T(1,128)}), f32[8,1,40960]{2,1,0:T(1,128)}, u32[]{:S(2)}, u32[]{:S(2)}) async-start(f32[8,1,40960]{2,1,0:T(1,128)} %reshape.13), calls=%async_computation | async-start | bytes 2621440 | tf_op jit(solution)/shard_map/all_to_all | solution.py:8
  92.6 400.6 %all-to-all-start.2 = ((f32[16,2,640,320]{2,3,1,0:T(8,128)}), f32[16,2,640,320]{2,3,1,0:T(8,128)}, u32[]{:S(2)}, u32[]{:S(2)}) async-start(f32[16,2,640,320]{2,3,1,0:T(8,128)} %stack.5), calls=%async_computation.2 | async-start | bytes 52428800 | tf_op jit(solution)/shard_map/all_to_all | solution.py:14
  99.4 490.3 %reduce-scatter.2.cloned.1.call-start = ((), (), s32[]{:S(2)}) async-start(), calls=%async_computation.4 | async-start | bytes 11796480 | tf_op jit(solution)/shard_map/reduce_scatter | solution.py:19
  531.2 58.5 %copy-start.1 = (f32[2,5120]{1,0:T(2,128)S(1)}, f32[2,5120]{1,0:T(2,128)}, u32[]{:S(2)}) copy-start(f32[2,5120]{1,0:T(2,128)} %param.7) | copy-start | bytes 122884
  531.2 58.5 %copy-start.2 = (f32[2,32]{1,0:T(2,128)S(1)}, f32[2,32]{1,0:T(2,128)}, u32[]{:S(2)}) copy-start(f32[2,32]{1,0:T(2,128)} %param.6) | copy-start | bytes 772
Sparse Core Ops, SparseCore 0:
  531.4 58.3 reduce-scatter.1
